TPU v7x, 256 devices: a whole 4x4x8 slice. The times are simulated.
256 devices in a mesh: doc: 32 (over y, x, core), term: 4 (over z_lo), pair: 2 (over z_hi).
Axes of the slice: x: 4, y: 4, z: 8 (z_hi: 2, z_lo: 4; z = z_hi * 4 + z_lo), core: 2. Of those that a mesh axis runs over, the one named last changes fastest.
Arguments:
- counts: int32 [64, 16, 128, 128], P('doc', 'term'), may hold values from 0 to 11
- block_ids: int32 [64, 16], P('doc', 'term'), may hold values from 0 to 8191, as said below
- live_slots: int32 [64, 16], P('doc', 'term'), may hold values 0 or 1
- lengths: int32 [8192], P('doc'), may hold values from 1 to 24528, as said below
- pairs: int32 [4096, 2], P(('doc', 'pair')), may hold values from 0 to 63, as said below
- pair_count: int32 [64], P(('doc', 'pair')), may hold values from 1 to 64, as said below
Outputs:
- gram: float32 [4096, 128, 128], P(('doc', 'pair'), 'term')
Inputs may be any that keep to these rules, and one draw needn't show every extreme that they name: `block_ids`: columns s * 4 to (s + 1) * 4 - 1 hold term blocks of the s-th of 4 equal ranges of the 8192 blocks, distinct within one document block and range. `lengths`: document b * 128 + r has a length of the sum of counts[b, s, r, t] over all slots s and all t plus tokens outside its blocks: 1 to 2000 of them for every document but the last, whose length is exactly 24528. `pairs`: the left block of row k belongs to doc index k // 128. Rows k with k % 64 < pair_count[k // 64] are live; some entry equals 64.
All inputs are finite; a program needn't handle non-finite values. No bound on the sum of `live_slots` on one device may be relied on, other than what follows from the above.
Results may differ from a plain program's by a relative error of at most 0.0014.
Values may be sent and summed in bfloat16 or wider, within the bound.
No kernel may reach another device: no remote copies, remote signals or barrier semaphores. Data moves between devices by JAX's collectives and lax.ppermute only.
A program may use at most 64 MiB of HBM per device.

v0:
```python
import jax
import jax.numpy as jnp
from jax import lax
from jax.sharding import PartitionSpec as P

V = 1048576
PB = 8
saturation = 1.2
length_weight = 0.75
epsilon = 1e-06


def gram_block(normalized, block_ids, whole_tiles, whole_ids, pair_batch, left_base):
    left_index = pair_batch[:, 0] - left_base
    right_pair_index = pair_batch[:, 1]
    left_tiles = normalized[left_index]
    right_tiles = whole_tiles[right_pair_index]
    matches = (block_ids[left_index][:, :, None] == whole_ids[right_pair_index][:, None, :]).astype(
        jnp.bfloat16
    )
    aligned = jnp.einsum(
        "pij,pjet->piet", matches, right_tiles, preferred_element_type=jnp.float32
    ).astype(jnp.bfloat16)
    return jnp.einsum("pidt,piet->pde", left_tiles, aligned, preferred_element_type=jnp.float32)


def run_pairs(work_pairs, work_count, normalized, block_ids, whole_tiles, whole_ids, left_base):
    capacity = work_pairs.shape[0]
    doc_rows = normalized.shape[2]
    step_count = (work_count + PB - 1) // PB

    def pair_step(loop_index, partial_value):
        first_row = loop_index * PB
        pair_batch = lax.dynamic_slice_in_dim(work_pairs, first_row, PB, 0)
        gram_tiles = gram_block(
            normalized, block_ids, whole_tiles, whole_ids, pair_batch, left_base
        )
        live_mask = first_row + jnp.arange(PB, dtype=jnp.int32) < work_count
        gram_tiles = jnp.where(live_mask[:, None, None], gram_tiles, 0.0)
        return lax.dynamic_update_slice_in_dim(partial_value, gram_tiles, first_row, 0)

    return lax.fori_loop(
        0, step_count, pair_step, jnp.zeros((capacity, doc_rows, doc_rows), jnp.float32)
    )


def shards(counts, block_ids, live_slots, lengths, pairs, pair_count):
    block_count, slot_count, doc_rows, term_columns = counts.shape
    covered_blocks = V // term_columns // lax.axis_size("term")
    local_ids = block_ids - lax.axis_index("term") * covered_blocks
    present = (counts > 0) & (live_slots[:, :, None, None] > 0)
    col_docs = jnp.sum(present.astype(jnp.float32), axis=2)
    freq_part = (
        jnp.zeros((covered_blocks, term_columns), jnp.float32)
        .at[local_ids.reshape(-1)]
        .add(col_docs.reshape(-1, term_columns))
    )
    len_float = lengths.astype(jnp.float32)
    doc_freq, len_total = (
        lax.psum(freq_part.astype(jnp.bfloat16), "doc").astype(jnp.float32),
        lax.psum(jnp.sum(len_float).astype(jnp.bfloat16), "doc").astype(jnp.float32),
    )
    docs_all = len_float.shape[0] * lax.axis_size("doc")
    avg_len = len_total / docs_all
    inv_freq = jnp.log(1.0 + (docs_all - doc_freq + 0.5) / (doc_freq + 0.5))
    slot_freq = inv_freq[local_ids]
    len_scale = (
        1.0
        - length_weight
        + length_weight * len_float.reshape(block_count, 1, doc_rows, 1) / avg_len
    )
    term_freq = counts.astype(jnp.float32)
    weight = jnp.where(
        present,
        slot_freq[:, :, None, :]
        * term_freq
        * (saturation + 1.0)
        / (term_freq + saturation * len_scale),
        0.0,
    )
    square_sum = lax.psum(jnp.sum(weight * weight, axis=(1, 3)), "term")
    normalized = (weight * lax.rsqrt(square_sum + epsilon)[:, None, :, None]).astype(jnp.bfloat16)
    whole_tiles, whole_ids = (
        lax.all_gather(normalized, "doc", axis=0, tiled=True),
        lax.all_gather(block_ids, "doc", axis=0, tiled=True),
    )
    left_base = lax.axis_index("doc") * block_count
    own_count = pair_count[0]
    partial_value = run_pairs(
        pairs, own_count, normalized, block_ids, whole_tiles, whole_ids, left_base
    )
    own_grams = lax.psum_scatter(partial_value, "term", scatter_dimension=1, tiled=True)
    return own_grams


def solution(mesh):
    in_specs = (
        P("doc", "term", None, None),
        P("doc", "term"),
        P("doc", "term"),
        P("doc"),
        P(("doc", "pair"), None),
        P(("doc", "pair")),
    )
    out_specs = P(("doc", "pair"), "term", None)
    return jax.shard_map(shards, mesh=mesh, in_specs=in_specs, out_specs=out_specs, check_vma=False)
```

profile of v0, /device:TPU:1, one launch (start us, length us, event | category | flops | bytes accessed | tf_op | source)
XLA Modules:
  0.0 361.6 jit_solution(16410767193192183070)
XLA Ops:
  6.5 0.7 broadcast_compare_fusion
  7.3 0.7 compare_select_fusion.2
  8.0 0.1 reshape.67
  8.1 1.2 convert_reduce_fusion
  9.2 0.9 scatter_custom_fusion
  10.1 0.8 convert_element_type.29
  11.0 0.0 all-reduce.2.cloned.1.call-update
  11.0 0.0 all-gather.3.cloned.1.call-start
  11.1 1.4 convert_reduce_fusion.1
  12.4 0.1 reshape.103
  12.5 65.9 %psum.22 = bf16[]{:T(256)} all-reduce(bf16[]{:T(256)} %convert_reduce_fusion.1), channel_id=1, replica_groups=mesh['doc'=32,'term'=4,'pair'=2] {'doc'}, use_global_device_ids=true, to_apply=%region_4.0 | all-reduce | flops 1 | bytes 4 | tf_op jit(solution)/shard_map/psum | solution.py:61
  79.1 0.7 multiply_bitcast_fusion
  79.8 49.5 %all-reduce.2.cloned.1.call-done = bf16[2048,128]{1,0:T(8,128)(2,1)} async-done(((bf16[2048,128]{1,0:T(8,128)(2,1)}), bf16[2048,128]{1,0:T(8,128)(2,1)}) %all-reduce.2.cloned.1.call-update) | async-done | bytes 524304 | tf_op jit(solution)/shard_map/psum | solution.py:60
  129.3 1.3 fusion.12
  130.7 0.6 gather_fusion.4
  131.2 0.4 multiply_reduce_fusion
  131.6 9.9 %psum.23 = f32[2,128]{1,0:T(2,128)S(1)} all-reduce(f32[2,128]{1,0:T(2,128)S(1)} %multiply_reduce_fusion), channel_id=1, replica_groups=mesh['doc'=32,'term'=4,'pair'=2] {'term'}, use_global_device_ids=true, to_apply=%region_6.7 | all-reduce | flops 256 | bytes 2048 | tf_op jit(solution)/shard_map/psum | solution.py:81
  141.5 1.0 multiply_convert_fusion
  142.6 0.0 reduce-scatter.2.cloned.1.call-start
  143.3 27.2 %all-gather = s32[32,2,4]{2,1,0:T(2,128)S(1)} all-gather(s32[1,2,4]{2,1,0:T(2,128)S(1)} %bitcast.35), channel_id=1, replica_groups=mesh['doc'=32,'term'=4,'pair'=2] {'doc'}, dimensions={0}, use_global_device_ids=true | all-gather | bytes 1056 | tf_op jit(solution)/shard_map/all_gather | solution.py:85
  170.6 29.1 %all-gather.3.cloned.1.call-done = bf16[64,4,128,128]{3,2,1,0:T(8,128)(2,1)} async-done(((bf16[2,4,128,128]{3,2,1,0:T(8,128)(2,1)}), bf16[64,4,128,128]{3,2,1,0:T(8,128)(2,1)}) %all-gather.3.cloned.1.call-update) | async-done | bytes 8388624 | tf_op jit(solution)/shard_map/all_gather | solution.py:84
  199.7 2.5 broadcast_in_dim.18
  202.2 9.1 %while.10 = (s32[]{:T(128)}, f32[64,128,128]{2,1,0:T(8,128)}, s32[]{:T(128)}, s32[]{:T(128)}, s32[64,2]{0,1:T(2,128)S(1)}, /*index=5*/s32[]{:T(128)}, bf16[2,4,1...) while((s32[]{:T(128)}, f32[64,128,128]{2,1,0:T(8,128)}, ...), condition=%wide.region_8.9_spmd, body=%wide.region_7.8_spmd.sunk | while | flops 138545360 | bytes 8922519 | solution.py:42
  202.2 0.7 add_compare_fusion.2
  202.8 0.1 constant_dynamic-slice_fusion.2
  202.9 0.6 gather_fusion.3
  203.5 0.6 gather_fusion.2
  204.1 4.1 %gather_fusion.1 = bf16[8,4,128,128]{3,2,1,0:T(8,128)(2,1)S(1)} fusion(bf16[64,4,128,128]{3,2,1,0:T(8,128)(2,1)} %get-tuple-element.192, s32[1024]{0:T(1024)S(1)} %get-tuple-element.154), kind=kCustom, calls=%fused_computation.3.clone.1 | custom fusion | bytes 2097184 | tf_op jit(solution)/shard_map/while/body/gather | solution.py:17
  208.2 1.0 fusion.27
  209.2 0.7 gather_fusion
  209.9 1.3 fusion.28
  211.3 143.8 %reduce-scatter.2.cloned.1.call-done = f32[64,32,128]{2,1,0:T(8,128)} async-done(((f32[64,128,128]{2,1,0:T(8,128)}), f32[64,32,128]{2,1,0:T(8,128)}) %reduce-scatter.2.cloned.1.call-update) | async-done | bytes 1048592 | tf_op jit(solution)/shard_map/reduce_scatter | solution.py:92
  (16 shorter events, 0.1 us)
Async XLA Ops:
  6.5 136.8 %copy-start.1 = (s32[2,4]{1,0:T(2,128)S(1)}, s32[2,4]{1,0:T(2,128)}, u32[]{:S(2)}) copy-start(s32[2,4]{1,0:T(2,128)} %param.9) | copy-start | bytes 100
  6.5 124.7 %copy-start.2 = (s32[2,4,128,128]{3,2,1,0:T(8,128)S(1)}, s32[2,4,128,128]{3,2,1,0:T(8,128)}, u32[]{:S(2)}) copy-start(s32[2,4,128,128]{3,2,1,0:T(8,128)} %param.8) | copy-start | bytes 1572868
  6.5 122.8 %all-reduce.2.cloned.1.call-start = ((), (), s32[]{:S(2)}) async-start(), calls=%async_computation.1 | async-start | bytes 1048576 | tf_op jit(solution)/shard_map/psum | solution.py:60
  11.0 191.2 %copy-start.3 = (s32[64,2]{0,1:T(2,128)S(1)}, s32[64,2]{0,1:T(2,128)}, u32[]{:S(2)}) copy-start(s32[64,2]{0,1:T(2,128)} %param.12) | copy-start | bytes 1540
  11.0 188.7 %all-gather.3.cloned.1.call-start = ((), (), s32[]{:S(2)}) async-start(), calls=%async_computation.2 | async-start | bytes 8650752 | tf_op jit(solution)/shard_map/all_gather | solution.py:84
  142.6 59.6 %copy-start = (bf16[2,4,128,128]{3,2,1,0:T(8,128)(2,1)S(1)}, bf16[2,4,128,128]{3,2,1,0:T(8,128)(2,1)}, u32[]{:S(2)}) copy-start(bf16[2,4,128,128]{3,2,1,0:T(8,128)(2,1)} %multiply_convert_fusion) | copy-start | bytes 786436
  142.6 212.5 %reduce-scatter.2.cloned.1.call-start = ((), (), s32[]{:S(2)}) async-start(), calls=%async_computation.3 | async-start | bytes 5242880 | tf_op jit(solution)/shard_map/reduce_scatter | solution.py:92
Sparse Core Ops, SparseCore 0:
  11.1 118.1 all-reduce.1
  142.7 56.9 all-gather.2
  211.4 143.6 reduce-scatter.1
where the time goes:
time: 362 us
  waiting for transfers between devices  222 us (61%)
  blocking collectives  103 us (28%)
  between operations  14.5 us (4%)
  other arithmetic  9.83 us (3%)
  local copies, waits for them, and re-layouts  9.29 us (3%)
    reduce_scatter x1, waiting for transfers between devices, shards(): lax.psum_scatter(partial_value, 'term', scatter_dimension=1, tiled=True)  144 us
    psum x1, blocking collectives, shards(): lax.psum(jnp.sum(len_float).astype(jnp.bfloat16), 'doc').astype(jnp.float32)  65.9 us
    psum x1, waiting for transfers between devices, shards(): lax.psum(freq_part.astype(jnp.bfloat16), 'doc').astype(jnp.float32)  49.5 us
    all_gather x1, waiting for transfers between devices, shards(): lax.all_gather(normalized, 'doc', axis=0, tiled=True)  29.1 us
    all_gather x1, blocking collectives, shards(): lax.all_gather(block_ids, 'doc', axis=0, tiled=True)  27.2 us
    psum x1, blocking collectives, shards(): square_sum = lax.psum(jnp.sum(weight * weight, axis=(1, 3)), 'term')  9.88 us
  transfers between devices with their start and end apart: 3, of which 3 were waited for; matrix products, arithmetic and copies ran while one was open for 1% of the time, Pallas kernels for 0%

commit v1 on v0

--- a/solution.py
+++ b/solution.py
@@ -2,12 +2,14 @@
 import jax.numpy as jnp
 from jax import lax
 from jax.sharding import PartitionSpec as P
+from jax.lax import all_gather
 
 V = 1048576
 PB = 8
 saturation = 1.2
 length_weight = 0.75
 epsilon = 1e-06
+point_the_page = lambda values: jnp.sum(all_gather(values, axis_name="doc"), axis=0)
 
 
 def gram_block(normalized, block_ids, whole_tiles, whole_ids, pair_batch, left_base):
@@ -57,7 +59,7 @@
     )
     len_float = lengths.astype(jnp.float32)
     doc_freq, len_total = (
-        lax.psum(freq_part.astype(jnp.bfloat16), "doc").astype(jnp.float32),
+        point_the_page(freq_part.astype(jnp.bfloat16)).astype(jnp.float32),
         lax.psum(jnp.sum(len_float).astype(jnp.bfloat16), "doc").astype(jnp.float32),
     )
     docs_all = len_float.shape[0] * lax.axis_size("doc")

time: 362 us -> 333 us (0.920)
  waiting for transfers between devices: 222 us -> 186 us
  other arithmetic: 9.83 us -> 17.4 us
    psum x1 -> x0, waiting for transfers between devices: 49.5 us -> none  [shards(): lax.psum(freq_part.astype(jnp.bfloat16), 'doc').astype(jnp.float32)]
    all_gather x0 -> x1, waiting for transfers between devices: none -> 12.4 us  [all_gather(values, axis_name='doc')]
    reduce_sum x0 -> x1, other arithmetic: none -> 8.78 us  [jnp.sum(all_gather(values, axis_name='doc'), axis=0)]
where the time goes in v1:
time: 333 us
  waiting for transfers between devices  186 us (56%)
  blocking collectives  103 us (31%)
  other arithmetic  17.4 us (5%)
  between operations  14.4 us (4%)
  local copies, waits for them, and re-layouts  9.29 us (3%)
    reduce_scatter x1, waiting for transfers between devices, shards(): lax.psum_scatter(partial_value, 'term', scatter_dimension=1, tiled=True)  144 us
    psum x1, blocking collectives, shards(): lax.psum(jnp.sum(len_float).astype(jnp.bfloat16), 'doc').astype(jnp.float32)  67.1 us
    all_gather x1, waiting for transfers between devices, shards(): lax.all_gather(normalized, 'doc', axis=0, tiled=True)  30.1 us
    all_gather x1, blocking collectives, shards(): lax.all_gather(block_ids, 'doc', axis=0, tiled=True)  25.7 us
    all_gather x1, waiting for transfers between devices, all_gather(values, axis_name='doc')  12.4 us
    psum x1, blocking collectives, shards(): square_sum = lax.psum(jnp.sum(weight * weight, axis=(1, 3)), 'term')  9.88 us
    reduce_sum x1, other arithmetic, jnp.sum(all_gather(values, axis_name='doc'), axis=0)  8.78 us
  transfers between devices with their start and end apart: 3, of which 3 were waited for; matrix products, arithmetic and copies ran while one was open for 1% of the time, Pallas kernels for 0%

profile of v1, /device:TPU:1, one launch (start us, length us, event | category | flops | bytes accessed | tf_op | source)
XLA Modules:
  0.0 332.6 jit_solution(5367118791989101572)
XLA Ops:
  6.5 0.7 broadcast_compare_fusion
  7.2 0.7 compare_select_fusion.2
  7.9 0.1 reshape.67
  8.0 1.2 convert_reduce_fusion
  9.2 0.9 scatter_custom_fusion
  10.1 0.8 convert_element_type.31
  10.9 0.0 all-gather.5.cloned.1.call-start
  11.0 1.3 convert_reduce_fusion.1
  12.3 67.1 %psum.14 = bf16[]{:T(256)} all-reduce(bf16[]{:T(256)} %convert_reduce_fusion.1), channel_id=1, replica_groups=mesh['doc'=32,'term'=4,'pair'=2] {'doc'}, use_global_device_ids=true, to_apply=%region_4.0 | all-reduce | flops 1 | bytes 4 | tf_op jit(solution)/shard_map/psum | solution.py:63
  79.4 0.1 reshape.103
  80.1 0.7 multiply_bitcast_fusion
  80.8 12.4 %all-gather.7.cloned.1.call-done = bf16[65536,128]{1,0:T(8,128)(2,1)} async-done(((bf16[2048,128]{1,0:T(8,128)(2,1)}), bf16[65536,128]{1,0:T(8,128)(2,1)}) %all-gather.7.cloned.1.call-update) | async-done | bytes 16777232 | tf_op jit(solution)/shard_map/all_gather | solution.py:12
  93.2 8.8 %reduce_sum.40 = bf16[2048,128]{1,0:T(8,128)(2,1)S(1)} reduce(bf16[32,2048,128]{2,1,0:T(8,128)(2,1)} %bitcast.37, bf16[]{:T(256)} %constant.25.clone.1), dimensions={0}, to_apply=%region_2.0 | reduce | flops 8126464 | bytes 17301506 | tf_op jit(solution)/shard_map/reduce_sum | solution.py:12
  102.0 0.3 fusion.12
  102.2 0.6 gather_fusion.4
  102.8 0.4 multiply_reduce_fusion
  103.2 9.9 %psum.15 = f32[2,128]{1,0:T(2,128)S(1)} all-reduce(f32[2,128]{1,0:T(2,128)S(1)} %multiply_reduce_fusion), channel_id=1, replica_groups=mesh['doc'=32,'term'=4,'pair'=2] {'term'}, use_global_device_ids=true, to_apply=%region_6.7 | all-reduce | flops 256 | bytes 2048 | tf_op jit(solution)/shard_map/psum | solution.py:83
  113.1 1.0 multiply_convert_fusion
  114.1 0.0 reduce-scatter.2.cloned.1.call-start
  114.9 25.7 %all-gather.1 = s32[32,2,4]{2,1,0:T(2,128)S(1)} all-gather(s32[1,2,4]{2,1,0:T(2,128)S(1)} %bitcast.36), channel_id=1, replica_groups=mesh['doc'=32,'term'=4,'pair'=2] {'doc'}, dimensions={0}, use_global_device_ids=true | all-gather | bytes 1056 | tf_op jit(solution)/shard_map/all_gather | solution.py:87
  140.6 30.1 %all-gather.5.cloned.1.call-done = bf16[64,4,128,128]{3,2,1,0:T(8,128)(2,1)} async-done(((bf16[2,4,128,128]{3,2,1,0:T(8,128)(2,1)}), bf16[64,4,128,128]{3,2,1,0:T(8,128)(2,1)}) %all-gather.5.cloned.1.call-update) | async-done | bytes 8388624 | tf_op jit(solution)/shard_map/all_gather | solution.py:86
  170.7 2.5 broadcast_in_dim.18
  173.2 9.0 %while.10 = (s32[]{:T(128)}, f32[64,128,128]{2,1,0:T(8,128)}, s32[]{:T(128)}, s32[]{:T(128)}, s32[64,2]{0,1:T(2,128)S(1)}, /*index=5*/s32[]{:T(128)}, bf16[2,4,1...) while((s32[]{:T(128)}, f32[64,128,128]{2,1,0:T(8,128)}, ...), condition=%wide.region_8.9_spmd, body=%wide.region_7.8_spmd.sunk | while | flops 139069648 | bytes 8922519 | solution.py:44
  173.2 0.7 add_compare_fusion.2
  173.9 0.1 constant_dynamic-slice_fusion.2
  174.0 0.6 gather_fusion.3
  174.5 0.6 gather_fusion.2
  175.1 4.1 %gather_fusion.1 = bf16[8,4,128,128]{3,2,1,0:T(8,128)(2,1)S(1)} fusion(bf16[64,4,128,128]{3,2,1,0:T(8,128)(2,1)} %get-tuple-element.192, s32[1024]{0:T(1024)S(1)} %get-tuple-element.154), kind=kCustom, calls=%fused_computation.3.clone.1 | custom fusion | bytes 2097184 | tf_op jit(solution)/shard_map/while/body/gather | solution.py:19
  179.2 1.0 convolution_convert_fusion.2
  180.2 0.7 gather_fusion
  180.9 1.3 fusion.28
  182.3 143.8 %reduce-scatter.2.cloned.1.call-done = f32[64,32,128]{2,1,0:T(8,128)} async-done(((f32[64,128,128]{2,1,0:T(8,128)}), f32[64,32,128]{2,1,0:T(8,128)}) %reduce-scatter.2.cloned.1.call-update) | async-done | bytes 1048592 | tf_op jit(solution)/shard_map/reduce_scatter | solution.py:94
  (17 shorter events, 0.1 us)
Async XLA Ops:
  6.5 86.6 %all-gather.7.cloned.1.call-start = ((), (), s32[]{:S(2)}) async-start(), calls=%async_computation.3 | async-start | bytes 17301504 | tf_op jit(solution)/shard_map/all_gather | solution.py:12
  10.9 159.8 %all-gather.5.cloned.1.call-start = ((), (), s32[]{:S(2)}) async-start(), calls=%async_computation.1 | async-start | bytes 8650752 | tf_op jit(solution)/shard_map/all_gather | solution.py:86
  93.2 9.7 %copy-start.2 = (s32[2,4,128,128]{3,2,1,0:T(8,128)S(1)}, s32[2,4,128,128]{3,2,1,0:T(8,128)}, u32[]{:S(2)}) copy-start(s32[2,4,128,128]{3,2,1,0:T(8,128)} %param.8) | copy-start | bytes 1572868
  93.2 21.7 %copy-start.1 = (s32[2,4]{1,0:T(2,128)S(1)}, s32[2,4]{1,0:T(2,128)}, u32[]{:S(2)}) copy-start(s32[2,4]{1,0:T(2,128)} %param.9) | copy-start | bytes 100
  101.9 71.3 %copy-start.3 = (s32[64,2]{0,1:T(2,128)S(1)}, s32[64,2]{0,1:T(2,128)}, u32[]{:S(2)}) copy-start(s32[64,2]{0,1:T(2,128)} %param.12) | copy-start | bytes 1540
  114.1 59.1 %copy-start = (bf16[2,4,128,128]{3,2,1,0:T(8,128)(2,1)S(1)}, bf16[2,4,128,128]{3,2,1,0:T(8,128)(2,1)}, u32[]{:S(2)}) copy-start(bf16[2,4,128,128]{3,2,1,0:T(8,128)(2,1)} %multiply_convert_fusion) | copy-start | bytes 786436
  114.1 211.9 %reduce-scatter.2.cloned.1.call-start = ((), (), s32[]{:S(2)}) async-start(), calls=%async_computation.2 | async-start | bytes 5242880 | tf_op jit(solution)/shard_map/reduce_scatter | solution.py:94
Sparse Core Ops, SparseCore 0:
  11.1 82.0 all-gather.6
  114.3 56.3 all-gather.4
  182.4 143.6 reduce-scatter.1
